TPU v7x, 32 devices: a whole 2x2x4 slice. The times are simulated.
32 devices in a mesh: kpt: 2 (over y), pert: 4 (over z), pw: 4 (over x, core).
Axes of the slice: x: 2, y: 2, z: 4, core: 2. Of those that a mesh axis runs over, the one named last changes fastest.
Arguments:
- occupied: bfloat16 [3072, 8192], P(('kpt', 'pert'), 'pw'), parts along dimension 0, may hold values from -0.0625 to 0.0625
- response: bfloat16 [8, 128, 8192], P(('kpt', 'pert'), None, 'pw'), parts along dimension 0, may hold values from -6 to 6
Outputs:
- correlation: float32 [8, 128, 1536], P(('kpt', 'pert')), parts along dimension 0
- projected: float32 [8, 128, 8192], P(('kpt', 'pert'), None, 'pw'), parts along dimension 0
There are 2 independent parts, one for each index of `kpt`. A program takes and returns all parts, laid end to end along the dimension named above; each array names one. Nothing has to cross between parts.
All inputs are finite; a program needn't handle non-finite values.
Results may differ from a plain program's by a relative error of at most 0.00096.
Values may be sent and summed in bfloat16 or wider, within the bound.
No kernel may reach another device: no remote copies, remote signals or barrier semaphores. Data moves between devices by JAX's collectives and lax.ppermute only.
A program may use at most 64 MiB of HBM per device.

v0:
```python
import jax
import jax.numpy as jnp
from jax import lax
from jax.sharding import PartitionSpec as P


def from_behind(block, axis, distance):
    devices = range(lax.axis_size(axis))
    route = [((i - distance) % len(devices), i) for i in devices]
    return lax.ppermute(block, axis, route)


def local(occupied, response):
    rows = response.reshape(-1, response.shape[-1])
    band_local = occupied.shape[0]
    cycle_size = lax.axis_size("pert")
    total_bands = band_local * cycle_size
    zero_index = jnp.zeros((), jnp.int32)
    empty_correlation = jnp.zeros((rows.shape[0], total_bands), jnp.float32)
    empty_correction = jnp.zeros(rows.shape, jnp.float32)
    position = lax.axis_index("pert")

    def visit(step, piece, correlation, correction):
        owner = (position - step) % cycle_size
        start = owner * band_local
        part = lax.dot_general(
            rows, piece, (((1,), (1,)), ((), ())), preferred_element_type=jnp.float32
        )
        summed = lax.psum(part, "pw")
        correlation = lax.dynamic_update_slice(correlation, summed, (zero_index, start))
        correction = correction + jnp.dot(
            summed.astype(jnp.bfloat16), piece, preferred_element_type=jnp.float32
        )
        return (correlation, correction)

    def turn(step, state):
        piece, correlation, correction = state
        correlation, correction = visit(step, piece, correlation, correction)
        piece = from_behind(piece, "pert", 1)
        return (piece, correlation, correction)

    piece, correlation, correction = lax.fori_loop(
        0, cycle_size - 1, turn, (occupied, empty_correlation, empty_correction)
    )
    correlation, correction = visit(cycle_size - 1, piece, correlation, correction)
    projected = rows.astype(jnp.float32) - correction
    correlation_out = correlation.reshape(response.shape[0], response.shape[1], total_bands)
    return (correlation_out, projected.reshape(response.shape))


def solution(mesh):
    in_specs = (P(("kpt", "pert"), "pw"), P(("kpt", "pert"), None, "pw"))
    out_specs = (P(("kpt", "pert"), None, None), P(("kpt", "pert"), None, "pw"))
    return jax.shard_map(local, mesh=mesh, in_specs=in_specs, out_specs=out_specs, check_vma=False)
```

profile of v0, /device:TPU:0, one launch (start us, length us, event | category | flops | bytes accessed | tf_op | source)
XLA Modules:
  0.0 176.5 jit_solution(3041188094833959325)
XLA Ops:
  8.0 1.0 broadcast_in_dim.6
  9.0 0.7 copy-done
  9.7 120.9 %while.20 = (s32[]{:T(128)}, bf16[384,2048]{1,0:T(8,128)(2,1)S(1)}, f32[128,1536]{1,0:T(8,128)}, f32[128,2048]{1,0:T(8,128)}, bf16[128,2048]{1,0:T(8,128)(2,1)},...) while((s32[]{:T(128)}, bf16[384,2048]{1,0:T(8,128)(2,1)S(1)}, ...), condition=%wide.region_2.3_spmd.clone, body=%wide.region_0.2_spmd.clone.sunk | while | flops 403275776 | bytes 19267988 | solution.py:42
  9.9 3.1 %collective-permute-start = (bf16[384,2048]{1,0:T(8,128)(2,1)S(1)}, bf16[384,2048]{1,0:T(8,128)(2,1)S(1)}, u32[]{:S(2)}, u32[]{:S(2)}) collective-permute-start(bf16[384,2048]{1,0:T(8,128)(2,1)S(1)} %copy.12), channel_id=1, source_target_pairs={{12,0},{0,4},{4,8},{8,12},{13,1},{1,5},{5,9},{9,13},{14,2},{2,6},{... | collective-permute-start | bytes 4718600 | tf_op jit(solution)/shard_map/while/body/eval_jaxpr/ppermute | solution.py:10
  13.0 1.3 fusion.20
  14.3 33.2 %all-reduce.5.cloned.1.call-done = f32[128,384]{1,0:T(8,128)} async-done(((f32[128,384]{1,0:T(8,128)}), f32[128,384]{1,0:T(8,128)}) %all-reduce.5.cloned.1.call-update) | async-done | bytes 196624 | tf_op jit(solution)/shard_map/while/body/eval_jaxpr/psum | solution.py:29
  47.6 1.6 constant_dynamic-update-slice_fusion.3
  49.2 2.3 %convolution_add_fusion.3 = f32[128,2048]{1,0:T(8,128)} fusion(bf16[384,2048]{1,0:T(8,128)(2,1)S(1)} %copy.12, f32[128,2048]{1,0:T(8,128)} %get-tuple-element.247, pred[]{:T(512)S(6)} %compare.5, f32[128,384]{1,0:T(8,128)} %all-reduce.5.cloned.1.call-done), kind=kOutput, calls=%fused_computation.clone.1 | convolution fusion | flops 201900032 | bytes 3866625 | tf_op jit(solution)/shard_map/while/body/eval_jaxpr/dot_general | solution.py:31
  51.5 0.2 copy.12
  51.7 1.5 collective-permute-start
  53.2 1.3 fusion.20
  54.6 32.1 %all-reduce.5.cloned.1.call-done = f32[128,384]{1,0:T(8,128)} async-done(((f32[128,384]{1,0:T(8,128)}), f32[128,384]{1,0:T(8,128)}) %all-reduce.5.cloned.1.call-update) | async-done | bytes 196624 | tf_op jit(solution)/shard_map/while/body/eval_jaxpr/psum | solution.py:29
  86.7 1.6 constant_dynamic-update-slice_fusion.3
  88.3 2.8 %convolution_add_fusion.3 = f32[128,2048]{1,0:T(8,128)} fusion(bf16[384,2048]{1,0:T(8,128)(2,1)S(1)} %copy.12, f32[128,2048]{1,0:T(8,128)} %get-tuple-element.247, pred[]{:T(512)S(6)} %compare.5, f32[128,384]{1,0:T(8,128)} %all-reduce.5.cloned.1.call-done), kind=kOutput, calls=%fused_computation.clone.1 | convolution fusion | flops 201900032 | bytes 3866625 | tf_op jit(solution)/shard_map/while/body/eval_jaxpr/dot_general | solution.py:31
  91.3 1.5 collective-permute-start
  92.8 1.3 fusion.20
  94.2 32.1 %all-reduce.5.cloned.1.call-done = f32[128,384]{1,0:T(8,128)} async-done(((f32[128,384]{1,0:T(8,128)}), f32[128,384]{1,0:T(8,128)}) %all-reduce.5.cloned.1.call-update) | async-done | bytes 196624 | tf_op jit(solution)/shard_map/while/body/eval_jaxpr/psum | solution.py:29
  126.3 1.6 constant_dynamic-update-slice_fusion.3
  127.9 2.8 %convolution_add_fusion.3 = f32[128,2048]{1,0:T(8,128)} fusion(bf16[384,2048]{1,0:T(8,128)(2,1)S(1)} %copy.12, f32[128,2048]{1,0:T(8,128)} %get-tuple-element.247, pred[]{:T(512)S(6)} %compare.5, f32[128,384]{1,0:T(8,128)} %all-reduce.5.cloned.1.call-done), kind=kOutput, calls=%fused_computation.clone.1 | convolution fusion | flops 201900032 | bytes 3866625 | tf_op jit(solution)/shard_map/while/body/eval_jaxpr/dot_general | solution.py:31
  130.7 2.4 %convolution_bitcast_fusion = f32[128,384]{0,1:T(8,128)} fusion(bf16[384,2048]{1,0:T(8,128)(2,1)S(1)} %get-tuple-element.160, bf16[1,128,2048]{2,1,0:T(8,128)(2,1)} %bitcast.22), kind=kOutput, calls=%fused_computation.6 | convolution fusion | flops 201326592 | bytes 2293760 | tf_op jit(solution)/shard_map/dot_general | solution.py:26
  133.1 32.1 %all-reduce.3.cloned.1.call-done = f32[128,384]{0,1:T(8,128)} async-done(((f32[128,384]{0,1:T(8,128)}), f32[128,384]{0,1:T(8,128)}) %all-reduce.3.cloned.1.call-update) | async-done | bytes 196624 | tf_op jit(solution)/shard_map/psum | solution.py:29
  165.3 1.1 copy.4
  166.3 0.7 constant_dynamic-update-slice_fusion.1
  167.0 2.4 %fusion.2 = f32[1,128,2048]{2,1,0:T(8,128)} fusion(f32[128,2048]{1,0:T(8,128)S(1)} %copy-done.1, bf16[384,2048]{1,0:T(8,128)(2,1)S(1)} %get-tuple-element.160, f32[128,384]{0,1:T(8,128)} %all-reduce.3.cloned.1.call-done, bf16[1,128,2048]{2,1,0:T(8,128)(2,1)S(1)} %bitcast.23), kind=kOutput, calls=%fused_computation.5 | convolution fusion | flops 202162176 | bytes 4390912 | tf_op jit(solution)/shard_map/dot_general | solution.py:31
  (25 shorter events, 0.4 us)
Async XLA Ops:
  8.0 1.7 copy-start
  9.7 37.9 %all-reduce.5.cloned.1.call-start = ((), (), s32[]{:S(2)}) async-start(), calls=%async_computation.1 | async-start | bytes 393216 | tf_op jit(solution)/shard_map/while/body/eval_jaxpr/psum | solution.py:29
  9.7 3.3 %copy-start.2 = (bf16[128,2048]{1,0:T(8,128)(2,1)S(1)}, bf16[128,2048]{1,0:T(8,128)(2,1)}, u32[]{:S(2)}) copy-start(bf16[128,2048]{1,0:T(8,128)(2,1)} %get-tuple-element.260) | copy-start | bytes 1572868 | tf_op jit(solution)/shard_map/while
  9.9 41.7 %collective-permute-start = (bf16[384,2048]{1,0:T(8,128)(2,1)S(1)}, bf16[384,2048]{1,0:T(8,128)(2,1)S(1)}, u32[]{:S(2)}, u32[]{:S(2)}) collective-permute-start(bf16[384,2048]{1,0:T(8,128)(2,1)S(1)} %copy.12), channel_id=1, source_target_pairs={{12,0},{0,4},{4,8},{8,12},{13,1},{1,5},{5,9},{9,13},{14,2},{2,6},{... | collective-permute-start | bytes 4718600 | tf_op jit(solution)/shard_map/while/body/eval_jaxpr/ppermute | solution.py:10
  51.5 35.2 %all-reduce.5.cloned.1.call-start = ((), (), s32[]{:S(2)}) async-start(), calls=%async_computation.1 | async-start | bytes 393216 | tf_op jit(solution)/shard_map/while/body/eval_jaxpr/psum | solution.py:29
  51.5 1.7 copy-start.2
  51.7 39.4 %collective-permute-start = (bf16[384,2048]{1,0:T(8,128)(2,1)S(1)}, bf16[384,2048]{1,0:T(8,128)(2,1)S(1)}, u32[]{:S(2)}, u32[]{:S(2)}) collective-permute-start(bf16[384,2048]{1,0:T(8,128)(2,1)S(1)} %copy.12), channel_id=1, source_target_pairs={{12,0},{0,4},{4,8},{8,12},{13,1},{1,5},{5,9},{9,13},{14,2},{2,6},{... | collective-permute-start | bytes 4718600 | tf_op jit(solution)/shard_map/while/body/eval_jaxpr/ppermute | solution.py:10
  91.1 35.2 %all-reduce.5.cloned.1.call-start = ((), (), s32[]{:S(2)}) async-start(), calls=%async_computation.1 | async-start | bytes 393216 | tf_op jit(solution)/shard_map/while/body/eval_jaxpr/psum | solution.py:29
  91.1 1.7 copy-start.2
  91.3 39.4 %collective-permute-start = (bf16[384,2048]{1,0:T(8,128)(2,1)S(1)}, bf16[384,2048]{1,0:T(8,128)(2,1)S(1)}, u32[]{:S(2)}, u32[]{:S(2)}) collective-permute-start(bf16[384,2048]{1,0:T(8,128)(2,1)S(1)} %copy.12), channel_id=1, source_target_pairs={{12,0},{0,4},{4,8},{8,12},{13,1},{1,5},{5,9},{9,13},{14,2},{2,6},{... | collective-permute-start | bytes 4718600 | tf_op jit(solution)/shard_map/while/body/eval_jaxpr/ppermute | solution.py:10
  130.6 34.6 %all-reduce.3.cloned.1.call-start = ((), (), s32[]{:S(2)}) async-start(), calls=%async_computation | async-start | bytes 393216 | tf_op jit(solution)/shard_map/psum | solution.py:29
  130.6 36.4 %copy-start.1 = (f32[128,2048]{1,0:T(8,128)S(1)}, f32[128,2048]{1,0:T(8,128)}, u32[]{:S(2)}) copy-start(f32[128,2048]{1,0:T(8,128)} %get-tuple-element.161) | copy-start | bytes 3145732
  130.6 36.4 %copy-start.3 = (bf16[128,2048]{1,0:T(8,128)(2,1)S(1)}, bf16[128,2048]{1,0:T(8,128)(2,1)}, u32[]{:S(2)}) copy-start(bf16[128,2048]{1,0:T(8,128)(2,1)} %get-tuple-element.272) | copy-start | bytes 1572868
Sparse Core Ops, SparseCore 0:
  14.4 33.0 all-reduce.4
  54.7 31.9 all-reduce.4
  94.2 31.9 all-reduce.4
Sparse Core Ops, SparseCore 1:
  133.4 31.8 all-reduce.2
where the time goes:
time: 177 us
  waiting for transfers between devices  130 us (73%)
  matrix products  16.5 us (9%)
  between operations  15.2 us (9%)
  local copies, waits for them, and re-layouts  8.78 us (5%)
  starting transfers between devices  6.19 us (3%)
    psum x4, waiting for transfers between devices, visit(): summed = lax.psum(part, 'pw')  130 us
    dot_general x4, matrix products, visit(): jnp.dot(summed.astype(jnp.bfloat16), piece, preferred_element_type=jnp.fl...  10.2 us
    dot_general x4, matrix products, visit(): lax.dot_general(rows, piece, (((1,), (1,)), ((), ())), preferred_element_...  6.32 us
    ppermute x3, starting transfers between devices, from_behind(): return lax.ppermute(block, axis, route)  6.18 us
    dynamic_update_slice x4, local copies, waits for them, and re-layouts, visit(): lax.dynamic_update_slice(correlation, summed, (zero_index, start))  5.54 us
  transfers between devices with their start and end apart: 7, of which 4 were waited for; matrix products, arithmetic and copies ran while one was open for 9% of the time, Pallas kernels for 0%

commit v1 on v0

v1 whole, which is shorter than its diff:
```python
import jax
import jax.numpy as jnp
from jax import lax
from jax.sharding import PartitionSpec as P


def shifted(block, axis, distance):
    size = lax.axis_size(axis)
    return lax.ppermute(block, axis, [(i, (i + distance) % size) for i in range(size)])


def partner(block, axis, mask):
    size = lax.axis_size(axis)
    return lax.ppermute(block, axis, [(i, i ^ mask) for i in range(size)])


def masks_of(size):
    return [1 << k for k in range(size.bit_length() - 1)]


def total(block, axis):
    size = lax.axis_size(axis)
    if size & (size - 1):
        return lax.psum(block, axis)
    for mask in masks_of(size):
        block = block + partner(block, axis, mask)
    return block


def local(occupied, response):
    rows = response.reshape(-1, response.shape[-1])
    height = rows.shape[0]
    bands = occupied.shape[0]
    ring = lax.axis_size("pert")
    slabs = lax.axis_size("pw")
    here = lax.axis_index("pert")
    slab = lax.axis_index("pw")

    def correlate(block):
        part = lax.dot_general(
            block, occupied, (((1,), (1,)), ((), ())), preferred_element_type=jnp.float32
        )
        largest = jnp.max(jnp.abs(block)).astype(jnp.float32)
        both = jnp.concatenate([part, jnp.full((8, bands), largest)], axis=0)
        both = total(both, "pw")
        return both[:height], both[height, 0]

    def correct(correlation):
        return jnp.dot(
            correlation.astype(jnp.bfloat16), occupied, preferred_element_type=jnp.float32
        )

    plane_waves = slabs * rows.shape[1]
    bound = bands * ring * plane_waves / 256.0 / 32768.0

    def factor(size):
        return jnp.where(size > 0, size, 1.0) * bound

    blocks = [rows]
    for _ in range(ring - 1):
        blocks.append(shifted(blocks[-1], "pert", 1))
    found = [correlate(block) for block in blocks]

    piece = height // slabs
    quarter = [lax.dynamic_slice_in_dim(c, slab * piece, piece, 0) for c, _ in found]
    gathered = jnp.zeros((piece, ring * bands), jnp.float32)
    for step in range(ring):
        got = quarter[step] if step == 0 else shifted(quarter[step], "pert", -step)
        gathered = lax.dynamic_update_slice(
            gathered, got, (jnp.zeros((), jnp.int32), (here + step) % ring * bands)
        )
    correlation = jnp.zeros((height, ring * bands), jnp.float32)
    correlation = lax.dynamic_update_slice_in_dim(correlation, gathered, slab * piece, 0)
    correlation = total(correlation, "pw") if slabs & (slabs - 1) else spread(gathered, slab, slabs)

    running = None
    for step in range(1, ring):
        c, size = found[step]
        added = correct(c) / factor(size)
        if running is not None:
            added = added + running.astype(jnp.float32)
        running = shifted(added.astype(jnp.float16), "pert", 1)
    correction = correct(found[0][0])
    if running is not None:
        correction = correction + running.astype(jnp.float32) * factor(found[0][1])
    projected = rows.astype(jnp.float32) - correction
    return (
        correlation.reshape(response.shape[0], response.shape[1], ring * bands),
        projected.reshape(response.shape),
    )


def spread(block, slab, slabs):
    for mask in masks_of(slabs):
        other = partner(block, "pw", mask)
        low = (slab & mask) == 0
        block = jnp.concatenate(
            [jnp.where(low, block, other), jnp.where(low, other, block)], axis=0
        )
    return block


def solution(mesh):
    in_specs = (P(("kpt", "pert"), "pw"), P(("kpt", "pert"), None, "pw"))
    out_specs = (P(("kpt", "pert"), None, None), P(("kpt", "pert"), None, "pw"))
    return jax.shard_map(local, mesh=mesh, in_specs=in_specs, out_specs=out_specs, check_vma=False)
```

time: 177 us -> 114 us (0.64)
  waiting for transfers between devices: 130 us -> 62.7 us
  other arithmetic: 0.01 us -> 11.6 us
  starting transfers between devices: 6.19 us -> 13.8 us
  between operations: 15.2 us -> 8.66 us
  matrix products: 16.5 us -> 10.7 us
  local copies, waits for them, and re-layouts: 8.78 us -> 6.28 us
    psum x4 -> x0, waiting for transfers between devices: 130 us -> none  [visit(): summed = lax.psum(part, 'pw')]
    ppermute x3 -> x19, waiting for transfers between devices: 0.01 us -> 62.7 us  [the longest x9 56.8 us: shifted(): lax.ppermute(block, axis, [(i, (i + distance) % size) for i in range(size)])]
    ppermute x3 -> x19, starting transfers between devices: 6.18 us -> 13.8 us  [the longest x9 7.36 us: shifted(): lax.ppermute(block, axis, [(i, (i + distance) % size) for i in range(size)])]
    dot_general x8, matrix products: 16.5 us -> 10.7 us  [the longest x4 7.3 us: correct(): jnp.dot(correlation.astype(jnp.bfloat16), occupied, preferred_element_typ...]
    dynamic_update_slice x4, local copies, waits for them, and re-layouts: 5.54 us -> 0.04 us  [local(): lax.dynamic_update_slice(gathered, got, (jnp.zeros((), jnp.int32), (here...]
    add x0 -> x8, other arithmetic: none -> 4.89 us  [total(): block = block + partner(block, axis, mask)]
    reduce_max x0 -> x4, other arithmetic: none -> 3.89 us  [correlate(): largest = jnp.max(jnp.abs(block)).astype(jnp.float32)]
    concatenate x0 -> x4, local copies, waits for them, and re-layouts: none -> 3.32 us  [correlate(): both = jnp.concatenate([part, jnp.full((8, bands), largest)], axis=0)]
  transfers between devices with their start and end apart: 7 -> 19, of which waited for: 4 -> 8; matrix products, arithmetic and copies ran while one was open for 9% -> 23% of each run, Pallas kernels for 0% -> 0%
where the time goes in v1:
time: 114 us
  waiting for transfers between devices  62.7 us (55%)
  starting transfers between devices  13.8 us (12%)
  other arithmetic  11.6 us (10%)
  matrix products  10.7 us (9%)
  between operations  8.66 us (8%)
  local copies, waits for them, and re-layouts  6.28 us (6%)
    ppermute x9, waiting for transfers between devices, shifted(): lax.ppermute(block, axis, [(i, (i + distance) % size) for i in range(size)])  56.8 us
    ppermute x9, starting transfers between devices, shifted(): lax.ppermute(block, axis, [(i, (i + distance) % size) for i in range(size)])  7.36 us
    dot_general x4, matrix products, correct(): jnp.dot(correlation.astype(jnp.bfloat16), occupied, preferred_element_typ...  7.3 us
    ppermute x10, starting transfers between devices, partner(): return lax.ppermute(block, axis, [(i, i ^ mask) for i in range(size)])  6.42 us
    ppermute x10, waiting for transfers between devices, partner(): return lax.ppermute(block, axis, [(i, i ^ mask) for i in range(size)])  5.87 us
    add x8, other arithmetic, total(): block = block + partner(block, axis, mask)  4.89 us
    reduce_max x4, other arithmetic, correlate(): largest = jnp.max(jnp.abs(block)).astype(jnp.float32)  3.89 us
    dot_general x4, matrix products, correlate(): lax.dot_general(block, occupied, (((1,), (1,)), ((), ())), preferred_elem...  3.42 us
  transfers between devices with their start and end apart: 19, of which 8 were waited for; matrix products, arithmetic and copies ran while one was open for 23% of the time, Pallas kernels for 0%

profile of v1, /device:TPU:0, one launch (start us, length us, event | category | flops | bytes accessed | tf_op | source)
XLA Modules:
  0.0 113.7 jit_solution(7672679786552781601)
XLA Ops:
  0.6 3.1 %collective-permute-start.2 = (bf16[128,2048]{1,0:T(8,128)(2,1)}, bf16[128,2048]{1,0:T(8,128)(2,1)S(1)}, u32[]{:S(2)}, u32[]{:S(2)}) collective-permute-start(bf16[128,2048]{1,0:T(8,128)(2,1)} %bitcast.24), channel_id=1, source_target_pairs={{0,4},{4,8},{8,12},{12,0},{1,5},{5,9},{9,13},{13,1},{2,6},{6,10},{... | collective-permute-start | bytes 1572872 | tf_op jit(solution)/shard_map/ppermute | solution.py:9
  3.7 1.8 %abs_reduce_fusion.3 = bf16[]{:T(256)} fusion(bf16[1,128,2048]{2,1,0:T(8,128)(2,1)} %param.3), kind=kLoop, calls=%fused_computation.15 | loop fusion | flops 524287 | bytes 524290 | tf_op jit(solution)/shard_map/reduce_max | solution.py:43
  5.5 1.6 %fusion.11 = f32[128,384]{1,0:T(8,128)S(1)} fusion(bf16[384,2048]{1,0:T(8,128)(2,1)S(1)} %copy-done, bf16[1,128,2048]{2,1,0:T(8,128)(2,1)} %param.3), kind=kOutput, calls=%fused_computation.32 | convolution fusion | flops 201326592 | bytes 2293760 | tf_op jit(solution)/shard_map/dot_general | solution.py:40
  8.5 9.4 %collective-permute-done.2 = bf16[128,2048]{1,0:T(8,128)(2,1)S(1)} collective-permute-done((bf16[128,2048]{1,0:T(8,128)(2,1)}, bf16[128,2048]{1,0:T(8,128)(2,1)S(1)}, u32[]{:S(2)}, u32[]{:S(2)}) %collective-permute-start.2) | collective-permute-done | bytes 524320 | tf_op jit(solution)/shard_map/ppermute | solution.py:9
  20.0 1.0 pad_add_fusion.3
  21.0 1.6 %collective-permute-start.1 = (f32[136,384]{1,0:T(8,128)S(1)}, f32[136,384]{1,0:T(8,128)}, u32[]{:S(2)}, u32[]{:S(2)}) collective-permute-start(f32[136,384]{1,0:T(8,128)S(1)} %pad_add_fusion.3), channel_id=1, source_target_pairs={{0,2},{1,3},{2,0},{3,1},{4,6},{5,7},{6,4},{7,5},{8,10},{9,11},{10,... | collective-permute-start | bytes 626696 | tf_op jit(solution)/shard_map/ppermute | solution.py:14
  24.8 8.7 %collective-permute-done.6 = bf16[128,2048]{1,0:T(8,128)(2,1)S(1)} collective-permute-done((bf16[128,2048]{1,0:T(8,128)(2,1)S(1)}, bf16[128,2048]{1,0:T(8,128)(2,1)S(1)}, u32[]{:S(2)}, u32[]{:S(2)}) %collective-permute-start.6) | collective-permute-done | bytes 524320 | tf_op jit(solution)/shard_map/ppermute | solution.py:9
  34.8 1.3 %concatenate.20 = f32[136,384]{1,0:T(8,128)} pad(f32[128,384]{1,0:T(8,128)S(1)} %fusion.18, bf16[]{:T(256)} %abs_reduce_fusion.1), padding=0_8x0_0 | pad | bytes 405506 | tf_op jit(solution)/shard_map/concatenate | solution.py:44
  37.8 1.0 add.87
  42.1 1.3 %collective-permute-start.8 = (f32[136,384]{1,0:T(8,128)S(1)}, f32[136,384]{1,0:T(8,128)S(1)}, u32[]{:S(2)}, u32[]{:S(2)}) collective-permute-start(f32[136,384]{1,0:T(8,128)S(1)} %pad_add_fusion.1), channel_id=1, source_target_pairs={{0,2},{1,3},{2,0},{3,1},{4,6},{5,7},{6,4},{7,5},{8,10},{9,11},{10,... | collective-permute-start | bytes 626696 | tf_op jit(solution)/shard_map/ppermute | solution.py:14
  43.4 1.2 %fusion.6 = f16[128,2048]{1,0:T(8,128)(2,1)} fusion(bf16[384,2048]{1,0:T(8,128)(2,1)S(1)} %copy-done, f32[]{:T(128)S(6)} %mul.43, f32[136,384]{1,0:T(8,128)S(1)} %add.87), kind=kOutput, calls=%fused_computation.10 | convolution fusion | flops 201850880 | bytes 2195460 | tf_op jit(solution)/shard_map/dot_general | solution.py:49
  44.8 3.9 %collective-permute-start.5 = (f32[32,384]{1,0:T(8,128)S(1)}, f32[32,384]{1,0:T(8,128)S(1)}, u32[]{:S(2)}, u32[]{:S(2)}) collective-permute-start(f32[32,384]{1,0:T(8,128)S(1)} %constant_dynamic-slice_fusion.2), channel_id=1, source_target_pairs={{0,12},{4,0},{8,4},{12,8},{1,13},{5,1},{9,5},{13,9},{2,14},{6,2},{... | collective-permute-start | bytes 147464 | tf_op jit(solution)/shard_map/ppermute | solution.py:9
  48.6 1.1 collective-permute-done.8
  51.7 6.1 %collective-permute-done.10 = bf16[128,2048]{1,0:T(8,128)(2,1)S(1)} collective-permute-done((bf16[128,2048]{1,0:T(8,128)(2,1)S(1)}, bf16[128,2048]{1,0:T(8,128)(2,1)S(1)}, u32[]{:S(2)}, u32[]{:S(2)}) %collective-permute-start.10) | collective-permute-done | bytes 524320 | tf_op jit(solution)/shard_map/ppermute | solution.py:9
  60.0 9.2 %collective-permute-done.16 = f16[128,2048]{1,0:T(8,128)(2,1)} collective-permute-done((f16[128,2048]{1,0:T(8,128)(2,1)}, f16[128,2048]{1,0:T(8,128)(2,1)}, u32[]{:S(2)}, u32[]{:S(2)}) %collective-permute-start.16) | collective-permute-done | bytes 524320 | tf_op jit(solution)/shard_map/ppermute | solution.py:9
  69.1 2.3 %fusion.5 = f16[128,2048]{1,0:T(8,128)(2,1)} fusion(bf16[384,2048]{1,0:T(8,128)(2,1)S(1)} %copy-done, f16[128,2048]{1,0:T(8,128)(2,1)} %collective-permute-done.16, f32[]{:T(128)S(6)} %mul.42, f32[136,384]{1,0:T(8,128)S(1)} %add.92), kind=kOutput, calls=%fused_computation.9 | convolution fusion | flops 202375168 | bytes 2719748 | tf_op jit(solution)/shard_map/dot_general | solution.py:49
  72.2 1.3 %collective-permute-start.12 = (f32[136,384]{1,0:T(8,128)S(1)}, f32[136,384]{1,0:T(8,128)S(1)}, u32[]{:S(2)}, u32[]{:S(2)}) collective-permute-start(f32[136,384]{1,0:T(8,128)S(1)} %pad_add_fusion), channel_id=1, source_target_pairs={{0,2},{1,3},{2,0},{3,1},{4,6},{5,7},{6,4},{7,5},{8,10},{9,11},{10,... | collective-permute-start | bytes 626696 | tf_op jit(solution)/shard_map/ppermute | solution.py:14
  73.7 4.8 %collective-permute-done.12 = f32[136,384]{1,0:T(8,128)S(1)} collective-permute-done((f32[136,384]{1,0:T(8,128)S(1)}, f32[136,384]{1,0:T(8,128)S(1)}, u32[]{:S(2)}, u32[]{:S(2)}) %collective-permute-start.12) | collective-permute-done | bytes 208928 | tf_op jit(solution)/shard_map/ppermute | solution.py:14
  78.6 11.0 %collective-permute-done.9 = f32[32,384]{1,0:T(8,128)S(1)} collective-permute-done((f32[32,384]{1,0:T(8,128)S(1)}, f32[32,384]{1,0:T(8,128)S(1)}, u32[]{:S(2)}, u32[]{:S(2)}) %collective-permute-start.9) | collective-permute-done | bytes 49184 | tf_op jit(solution)/shard_map/ppermute | solution.py:9
  91.6 2.3 %fusion.4 = f16[128,2048]{1,0:T(8,128)(2,1)} fusion(bf16[384,2048]{1,0:T(8,128)(2,1)S(1)} %copy-done, f16[128,2048]{1,0:T(8,128)(2,1)} %collective-permute-done.17, f32[]{:T(128)S(6)} %mul.41, f32[136,384]{1,0:T(8,128)S(1)} %add.97), kind=kOutput, calls=%fused_computation.8 | convolution fusion | flops 202375168 | bytes 2719748 | tf_op jit(solution)/shard_map/dot_general | solution.py:49
  94.7 1.3 %collective-permute-start.15 = (f32[64,1536]{1,0:T(8,128)}, f32[64,1536]{1,0:T(8,128)}, u32[]{:S(2)}, u32[]{:S(2)}) collective-permute-start(f32[64,1536]{1,0:T(8,128)} %pad_maximum_fusion), channel_id=1, source_target_pairs={{0,2},{1,3},{2,0},{3,1},{4,6},{5,7},{6,4},{7,5},{8,10},{9,11},{10,... | collective-permute-start | bytes 1179656 | tf_op jit(solution)/shard_map/ppermute | solution.py:14
  97.8 12.4 %collective-permute-done.18 = f16[128,2048]{1,0:T(8,128)(2,1)S(1)} collective-permute-done((f16[128,2048]{1,0:T(8,128)(2,1)}, f16[128,2048]{1,0:T(8,128)(2,1)S(1)}, u32[]{:S(2)}, u32[]{:S(2)}) %collective-permute-start.18) | collective-permute-done | bytes 524320 | tf_op jit(solution)/shard_map/ppermute | solution.py:9
  110.2 1.4 %fusion.3 = f32[1,128,2048]{2,1,0:T(8,128)} fusion(bf16[384,2048]{1,0:T(8,128)(2,1)S(1)} %copy-done, f16[128,2048]{1,0:T(8,128)(2,1)S(1)} %collective-permute-done.18, f32[]{:T(128)S(6)} %mul.44, bf16[1,128,2048]{2,1,0:T(8,128)(2,1)S(1)} %copy-done.1, f32[136,384]{1,0:T(8,128)S(1)} %add.82), kind=kOutput, calls=%fused_computation.7 | convolution fusion | flops 202637312 | bytes 3768324 | tf_op jit(solution)/shard_map/dot_general | solution.py:49
  111.7 1.1 broadcast_select_fusion.1
  (66 shorter events, 14.9 us)
Async XLA Ops:
  0.6 4.9 %copy-start = (bf16[384,2048]{1,0:T(8,128)(2,1)S(1)}, bf16[384,2048]{1,0:T(8,128)(2,1)}, u32[]{:S(2)}) copy-start(bf16[384,2048]{1,0:T(8,128)(2,1)} %param.2) | copy-start | bytes 4718596
  0.6 17.3 %collective-permute-start.2 = (bf16[128,2048]{1,0:T(8,128)(2,1)}, bf16[128,2048]{1,0:T(8,128)(2,1)S(1)}, u32[]{:S(2)}, u32[]{:S(2)}) collective-permute-start(bf16[128,2048]{1,0:T(8,128)(2,1)} %bitcast.24), channel_id=1, source_target_pairs={{0,4},{4,8},{8,12},{12,0},{1,5},{5,9},{9,13},{13,1},{2,6},{6,10},{... | collective-permute-start | bytes 1572872 | tf_op jit(solution)/shard_map/ppermute | solution.py:9
  7.8 12.2 %collective-permute-start = (f32[136,384]{1,0:T(8,128)S(1)}, f32[136,384]{1,0:T(8,128)}, u32[]{:S(2)}, u32[]{:S(2)}) collective-permute-start(f32[136,384]{1,0:T(8,128)S(1)} %concatenate.18), channel_id=1, source_target_pairs={{0,1},{1,0},{2,3},{3,2},{4,5},{5,4},{6,7},{7,6},{8,9},{9,8},{10,11... | collective-permute-start | bytes 626696 | tf_op jit(solution)/shard_map/ppermute | solution.py:14
  18.5 14.9 %collective-permute-start.6 = (bf16[128,2048]{1,0:T(8,128)(2,1)S(1)}, bf16[128,2048]{1,0:T(8,128)(2,1)S(1)}, u32[]{:S(2)}, u32[]{:S(2)}) collective-permute-start(bf16[128,2048]{1,0:T(8,128)(2,1)S(1)} %collective-permute-done.2), channel_id=1, source_target_pairs={{0,4},{4,8},{8,12},{12,0},{1,5},{5,9},{9,13},{13,1},{2,6},{6,10},{... | collective-permute-start | bytes 1572872 | tf_op jit(solution)/shard_map/ppermute | solution.py:9
  19.9 3.3 %collective-permute-start.3 = (f32[136,384]{1,0:T(8,128)S(1)}, f32[136,384]{1,0:T(8,128)}, u32[]{:S(2)}, u32[]{:S(2)}) collective-permute-start(f32[136,384]{1,0:T(8,128)S(1)} %concatenate.19), channel_id=1, source_target_pairs={{0,1},{1,0},{2,3},{3,2},{4,5},{5,4},{6,7},{7,6},{8,9},{9,8},{10,11... | collective-permute-start | bytes 626696 | tf_op jit(solution)/shard_map/ppermute | solution.py:14
  21.0 15.1 %collective-permute-start.1 = (f32[136,384]{1,0:T(8,128)S(1)}, f32[136,384]{1,0:T(8,128)}, u32[]{:S(2)}, u32[]{:S(2)}) collective-permute-start(f32[136,384]{1,0:T(8,128)S(1)} %pad_add_fusion.3), channel_id=1, source_target_pairs={{0,2},{1,3},{2,0},{3,1},{4,6},{5,7},{6,4},{7,5},{8,10},{9,11},{10,... | collective-permute-start | bytes 626696 | tf_op jit(solution)/shard_map/ppermute | solution.py:14
  24.2 13.7 %collective-permute-start.4 = (f32[136,384]{1,0:T(8,128)S(1)}, f32[136,384]{1,0:T(8,128)}, u32[]{:S(2)}, u32[]{:S(2)}) collective-permute-start(f32[136,384]{1,0:T(8,128)S(1)} %pad_add_fusion.2), channel_id=1, source_target_pairs={{0,2},{1,3},{2,0},{3,1},{4,6},{5,7},{6,4},{7,5},{8,10},{9,11},{10,... | collective-permute-start | bytes 626696 | tf_op jit(solution)/shard_map/ppermute | solution.py:14
  36.1 5.0 %collective-permute-start.7 = (f32[136,384]{1,0:T(8,128)}, f32[136,384]{1,0:T(8,128)}, u32[]{:S(2)}, u32[]{:S(2)}) collective-permute-start(f32[136,384]{1,0:T(8,128)} %concatenate.20), channel_id=1, source_target_pairs={{0,1},{1,0},{2,3},{3,2},{4,5},{5,4},{6,7},{7,6},{8,9},{9,8},{10,11... | collective-permute-start | bytes 626696 | tf_op jit(solution)/shard_map/ppermute | solution.py:14
  37.1 0.7 copy-start.2
  41.1 16.8 %collective-permute-start.10 = (bf16[128,2048]{1,0:T(8,128)(2,1)S(1)}, bf16[128,2048]{1,0:T(8,128)(2,1)S(1)}, u32[]{:S(2)}, u32[]{:S(2)}) collective-permute-start(bf16[128,2048]{1,0:T(8,128)(2,1)S(1)} %collective-permute-done.6), channel_id=1, source_target_pairs={{0,4},{4,8},{8,12},{12,0},{1,5},{5,9},{9,13},{13,1},{2,6},{6,10},{... | collective-permute-start | bytes 1572872 | tf_op jit(solution)/shard_map/ppermute | solution.py:9
  42.1 7.6 %collective-permute-start.8 = (f32[136,384]{1,0:T(8,128)S(1)}, f32[136,384]{1,0:T(8,128)S(1)}, u32[]{:S(2)}, u32[]{:S(2)}) collective-permute-start(f32[136,384]{1,0:T(8,128)S(1)} %pad_add_fusion.1), channel_id=1, source_target_pairs={{0,2},{1,3},{2,0},{3,1},{4,6},{5,7},{6,4},{7,5},{8,10},{9,11},{10,... | collective-permute-start | bytes 626696 | tf_op jit(solution)/shard_map/ppermute | solution.py:14
  44.7 24.4 %collective-permute-start.16 = (f16[128,2048]{1,0:T(8,128)(2,1)}, f16[128,2048]{1,0:T(8,128)(2,1)}, u32[]{:S(2)}, u32[]{:S(2)}) collective-permute-start(f16[128,2048]{1,0:T(8,128)(2,1)} %fusion.6), channel_id=1, source_target_pairs={{0,4},{4,8},{8,12},{12,0},{1,5},{5,9},{9,13},{13,1},{2,6},{6,10},{... | collective-permute-start | bytes 1572872 | tf_op jit(solution)/shard_map/ppermute | solution.py:9
  44.8 28.7 %collective-permute-start.5 = (f32[32,384]{1,0:T(8,128)S(1)}, f32[32,384]{1,0:T(8,128)S(1)}, u32[]{:S(2)}, u32[]{:S(2)}) collective-permute-start(f32[32,384]{1,0:T(8,128)S(1)} %constant_dynamic-slice_fusion.2), channel_id=1, source_target_pairs={{0,12},{4,0},{8,4},{12,8},{1,13},{5,1},{9,5},{13,9},{2,14},{6,2},{... | collective-permute-start | bytes 147464 | tf_op jit(solution)/shard_map/ppermute | solution.py:9
  59.9 13.6 %copy-start.3 = (f32[32,1536]{1,0:T(8,128)S(1)}, f32[32,1536]{1,0:T(8,128)}, u32[]{:S(2)}) copy-start(f32[32,1536]{1,0:T(8,128)} %copy-done.2) | copy-start | bytes 589828
  59.9 12.2 %collective-permute-start.11 = (f32[136,384]{1,0:T(8,128)S(1)}, f32[136,384]{1,0:T(8,128)S(1)}, u32[]{:S(2)}, u32[]{:S(2)}) collective-permute-start(f32[136,384]{1,0:T(8,128)S(1)} %concatenate.21), channel_id=1, source_target_pairs={{0,1},{1,0},{2,3},{3,2},{4,5},{5,4},{6,7},{7,6},{8,9},{9,8},{10,11... | collective-permute-start | bytes 626696 | tf_op jit(solution)/shard_map/ppermute | solution.py:14
  71.4 20.1 %collective-permute-start.17 = (f16[128,2048]{1,0:T(8,128)(2,1)}, f16[128,2048]{1,0:T(8,128)(2,1)}, u32[]{:S(2)}, u32[]{:S(2)}) collective-permute-start(f16[128,2048]{1,0:T(8,128)(2,1)} %fusion.5), channel_id=1, source_target_pairs={{0,4},{4,8},{8,12},{12,0},{1,5},{5,9},{9,13},{13,1},{2,6},{6,10},{... | collective-permute-start | bytes 1572872 | tf_op jit(solution)/shard_map/ppermute | solution.py:9
  72.2 6.3 %collective-permute-start.12 = (f32[136,384]{1,0:T(8,128)S(1)}, f32[136,384]{1,0:T(8,128)S(1)}, u32[]{:S(2)}, u32[]{:S(2)}) collective-permute-start(f32[136,384]{1,0:T(8,128)S(1)} %pad_add_fusion), channel_id=1, source_target_pairs={{0,2},{1,3},{2,0},{3,1},{4,6},{5,7},{6,4},{7,5},{8,10},{9,11},{10,... | collective-permute-start | bytes 626696 | tf_op jit(solution)/shard_map/ppermute | solution.py:14
  73.6 16.1 %collective-permute-start.9 = (f32[32,384]{1,0:T(8,128)S(1)}, f32[32,384]{1,0:T(8,128)S(1)}, u32[]{:S(2)}, u32[]{:S(2)}) collective-permute-start(f32[32,384]{1,0:T(8,128)S(1)} %constant_dynamic-slice_fusion.1), channel_id=1, source_target_pairs={{0,8},{4,12},{8,0},{12,4},{1,9},{5,13},{9,1},{13,5},{2,10},{6,14},... | collective-permute-start | bytes 147464 | tf_op jit(solution)/shard_map/ppermute | solution.py:9
  78.6 12.9 %collective-permute-start.13 = (f32[32,384]{1,0:T(8,128)S(1)}, f32[32,384]{1,0:T(8,128)S(1)}, u32[]{:S(2)}, u32[]{:S(2)}) collective-permute-start(f32[32,384]{1,0:T(8,128)S(1)} %constant_dynamic-slice_fusion), channel_id=1, source_target_pairs={{0,4},{4,8},{8,12},{12,0},{1,5},{5,9},{9,13},{13,1},{2,6},{6,10},{... | collective-permute-start | bytes 147464 | tf_op jit(solution)/shard_map/ppermute | solution.py:9
  91.5 2.4 %collective-permute-start.14 = (f32[32,1536]{1,0:T(8,128)S(1)}, f32[32,1536]{1,0:T(8,128)S(1)}, u32[]{:S(2)}, u32[]{:S(2)}) collective-permute-start(f32[32,1536]{1,0:T(8,128)S(1)} %constant_dynamic-update-slice_fusion.2), channel_id=1, source_target_pairs={{0,1},{1,0},{2,3},{3,2},{4,5},{5,4},{6,7},{7,6},{8,9},{9,8},{10,11... | collective-permute-start | bytes 589832 | tf_op jit(solution)/shard_map/ppermute | solution.py:14
  93.9 16.3 %copy-start.1 = (bf16[1,128,2048]{2,1,0:T(8,128)(2,1)S(1)}, bf16[1,128,2048]{2,1,0:T(8,128)(2,1)}, u32[]{:S(2)}) copy-start(bf16[1,128,2048]{2,1,0:T(8,128)(2,1)} %param.3) | copy-start | bytes 1572868
  93.9 16.3 %collective-permute-start.18 = (f16[128,2048]{1,0:T(8,128)(2,1)}, f16[128,2048]{1,0:T(8,128)(2,1)S(1)}, u32[]{:S(2)}, u32[]{:S(2)}) collective-permute-start(f16[128,2048]{1,0:T(8,128)(2,1)} %fusion.4), channel_id=1, source_target_pairs={{0,4},{4,8},{8,12},{12,0},{1,5},{5,9},{9,13},{13,1},{2,6},{6,10},{... | collective-permute-start | bytes 1572872 | tf_op jit(solution)/shard_map/ppermute | solution.py:9
  94.7 17.0 %collective-permute-start.15 = (f32[64,1536]{1,0:T(8,128)}, f32[64,1536]{1,0:T(8,128)}, u32[]{:S(2)}, u32[]{:S(2)}) collective-permute-start(f32[64,1536]{1,0:T(8,128)} %pad_maximum_fusion), channel_id=1, source_target_pairs={{0,2},{1,3},{2,0},{3,1},{4,6},{5,7},{6,4},{7,5},{8,10},{9,11},{10,... | collective-permute-start | bytes 1179656 | tf_op jit(solution)/shard_map/ppermute | solution.py:14
